TPU v7x, 32 devices: a whole 2x2x4 slice. The times are simulated.
32 devices in a mesh: dp: 8 (over z, core), expert: 4 (over y, x).
Axes of the slice: x: 2, y: 2, z: 4, core: 2. Of those that a mesh axis runs over, the one named last changes fastest.
Arguments:
- tokens: bfloat16 [24576, 2048], P(('dp', 'expert')), may hold values from -6 to 6
- target: bfloat16 [24576, 2048], P(('dp', 'expert')), may hold values from -4 to 4
- route_index: int32 [8, 4, 4, 16], P('dp', None, 'expert'), may hold values from 0 to 767, as said below
- route_count: int32 [8, 4, 4], P('dp', None, 'expert'), may hold values from 1 to 16, as said below
- route_gate: float32 [8, 4, 4, 16], P('dp', None, 'expert'), may hold values from 0.1 to 1
- gate_weight: bfloat16 [2048, 4, 768], P('dp', 'expert'), may hold values from -0.125 to 0.125
- up_weight: bfloat16 [2048, 4, 768], P('dp', 'expert'), may hold values from -0.125 to 0.125
- down_weight: bfloat16 [2048, 4, 768], P('dp', 'expert'), may hold values from -0.21875 to 0.21875
Outputs:
- token_grad: bfloat16 [24576, 2048], P(('dp', 'expert'))
- gate_gradient: float32 [2048, 4, 768], P('dp', 'expert')
- up_gradient: float32 [2048, 4, 768], P('dp', 'expert')
- down_gradient: float32 [2048, 4, 768], P('dp', 'expert')
Inputs may be any that keep to these rules, and one draw needn't show every extreme that they name: `route_index`: within each list of 16 slots the indices are distinct; each names a token of the source device. `route_count`: in every group one expert has all 16 slots live from every source device; slots at or beyond the count are unused.
All inputs are finite; a program needn't handle non-finite values.
Results may differ from a plain program's by a relative error of at most 0.0059.
Values may be sent and summed in bfloat16 or wider, within the bound.
A program may use at most 128 MiB of HBM per device.

v0:
```python
import jax
import jax.numpy as jnp
from jax import lax
from jax.sharding import PartitionSpec as P


def to_owners(block):
    return lax.all_to_all(block, "expert", split_axis=0, concat_axis=1, tiled=True)


def to_sources(block):
    return lax.all_to_all(block, "expert", split_axis=1, concat_axis=0, tiled=True)


def on_device(
    tokens, target, route_index, route_count, route_gate, gate_weight, up_weight, down_weight
):
    groups = lax.axis_size("dp")
    sources = lax.axis_size("expert")
    local_index = route_index[0, :, 0, :]
    live_count = route_count[0, :, 0]
    per_source = local_index.shape[1]
    model_width = tokens.shape[1]
    usable = jnp.arange(per_source, dtype=jnp.int32)[None, :] < live_count[:, None]
    slot_weight = jnp.where(usable, route_gate[0, :, 0, :], 0.0)
    outgoing = tokens[local_index] * usable[:, :, None].astype(tokens.dtype)
    expert_rows = to_owners(outgoing)
    full_gate, full_up, full_down = (
        lax.all_gather(gate_weight, "dp", axis=0, tiled=True),
        lax.all_gather(up_weight, "dp", axis=0, tiled=True),
        lax.all_gather(down_weight, "dp", axis=0, tiled=True),
    )
    gate_pre = jnp.einsum(
        "erd,def->erf", expert_rows, full_gate, preferred_element_type=jnp.float32
    )
    up_pre = jnp.einsum("erd,def->erf", expert_rows, full_up, preferred_element_type=jnp.float32)
    sigma = jax.nn.sigmoid(gate_pre)
    active = gate_pre * sigma
    hidden = (active * up_pre).astype(jnp.bfloat16)
    expert_out = jnp.einsum(
        "erf,def->erd", hidden, full_down, preferred_element_type=jnp.float32
    ).astype(jnp.bfloat16)
    returned = to_sources(expert_out)
    flat_index = local_index.reshape(-1)
    combined = (
        jnp.zeros((tokens.shape[0], model_width), jnp.float32)
        .at[flat_index]
        .add((slot_weight[:, :, None] * returned.astype(jnp.float32)).reshape(-1, model_width))
    )
    out_grad = combined - target.astype(jnp.float32)
    slot_grad = (slot_weight[:, :, None] * out_grad[local_index]).astype(jnp.bfloat16)
    owner_grad = to_owners(slot_grad)
    hidden_grad = jnp.einsum(
        "erd,def->erf", owner_grad, full_down, preferred_element_type=jnp.float32
    )
    gate_grad = (hidden_grad * up_pre * sigma * (1.0 + gate_pre * (1.0 - sigma))).astype(
        jnp.bfloat16
    )
    up_grad = (hidden_grad * active).astype(jnp.bfloat16)
    row_grad = (
        jnp.einsum("erf,def->erd", gate_grad, full_gate, preferred_element_type=jnp.float32)
        + jnp.einsum("erf,def->erd", up_grad, full_up, preferred_element_type=jnp.float32)
    ).astype(jnp.bfloat16)
    came_back = to_sources(row_grad)
    token_grad = (
        jnp.zeros((tokens.shape[0], model_width), jnp.float32)
        .at[flat_index]
        .add(came_back.astype(jnp.float32).reshape(-1, model_width))
        .astype(jnp.bfloat16)
    )
    factor = (groups * sources * per_source) ** (-0.5)
    rows_every, grad_every = (
        lax.all_to_all(expert_rows, "dp", split_axis=2, concat_axis=1, tiled=True),
        lax.all_to_all(owner_grad, "dp", split_axis=2, concat_axis=1, tiled=True),
    )
    hidden_piece = lax.all_gather(hidden, "dp", axis=1, tiled=True)
    gate_piece = lax.all_gather(gate_grad, "dp", axis=1, tiled=True)
    up_piece = lax.all_gather(up_grad, "dp", axis=1, tiled=True)
    gate_sum = jnp.einsum(
        "erd,erf->def", rows_every, gate_piece, preferred_element_type=jnp.float32
    )
    up_sum = jnp.einsum("erd,erf->def", rows_every, up_piece, preferred_element_type=jnp.float32)
    down_sum = jnp.einsum(
        "erd,erf->def", grad_every, hidden_piece, preferred_element_type=jnp.float32
    )
    gate_gradient = gate_sum * factor
    up_gradient = up_sum * factor
    down_gradient = down_sum * factor
    return (token_grad, gate_gradient, up_gradient, down_gradient)


def solution(mesh):
    return jax.shard_map(
        on_device,
        mesh=mesh,
        in_specs=(
            P(("dp", "expert"), None),
            P(("dp", "expert"), None),
            P("dp", None, "expert", None),
            P("dp", None, "expert"),
            P("dp", None, "expert", None),
            P("dp", "expert", None),
            P("dp", "expert", None),
            P("dp", "expert", None),
        ),
        out_specs=(
            P(("dp", "expert"), None),
            P("dp", "expert", None),
            P("dp", "expert", None),
            P("dp", "expert", None),
        ),
        check_vma=False,
    )
```

profile of v0, /device:TPU:0, one launch (start us, length us, event | category | flops | bytes accessed | tf_op | source)
XLA Modules:
  0.0 305.2 jit_solution(9919206521907058066)
XLA Ops:
  11.8 5.2 %all-to-all-start = ((bf16[4,16,2048]{2,1,0:T(8,128)(2,1)}), bf16[4,16,2048]{2,1,0:T(8,128)(2,1)S(1)}, u32[]{:S(2)}, u32[]{:S(2)}) async-start(bf16[4,16,2048]{2,1,0:T(8,128)(2,1)} %broadcast_multiply_fusion), calls=%async_computation | async-start | bytes 524288 | tf_op jit(solution)/shard_map/all_to_all | solution.py:8
  18.3 4.1 %all-to-all-done = bf16[4,16,2048]{2,1,0:T(8,128)(2,1)S(1)} async-done(((bf16[4,16,2048]{2,1,0:T(8,128)(2,1)}), bf16[4,16,2048]{2,1,0:T(8,128)(2,1)S(1)}, u32[]{:S(2)}, u32[]{:S(2)}) %all-to-all-start) | async-done | bytes 262176 | tf_op jit(solution)/shard_map/all_to_all | solution.py:8
  24.9 13.3 %reduce.10 = bf16[2048,64]{1,0:T(8,128)(2,1)} reduce(bf16[2048,1,64]{2,1,0:T(2,128)(2,1)} %bitcast.114, bf16[]{:T(256)} %broadcast.134), dimensions={1}, to_apply=%bitcast.86.reduce_sub_computation | reduce | bytes 524290
  40.3 4.9 %all-to-all-start.4 = ((bf16[8,2,8192]{2,1,0:T(2,128)(2,1)}), bf16[8,2,8192]{2,1,0:T(2,128)(2,1)}, u32[]{:S(2)}, u32[]{:S(2)}) async-start(bf16[8,2,8192]{2,1,0:T(2,128)(2,1)} %reshape.301), calls=%async_computation.4 | async-start | bytes 524288 | tf_op jit(solution)/shard_map/all_to_all | solution.py:73
  46.6 8.4 %all-to-all-done.4 = bf16[8,2,8192]{2,1,0:T(2,128)(2,1)} async-done(((bf16[8,2,8192]{2,1,0:T(2,128)(2,1)}), bf16[8,2,8192]{2,1,0:T(2,128)(2,1)}, u32[]{:S(2)}, u32[]{:S(2)}) %all-to-all-start.4) | async-done | bytes 262176 | tf_op jit(solution)/shard_map/all_to_all | solution.py:73
  58.4 3.4 %copy.41 = bf16[1,64,2048]{2,1,0:T(8,128)(2,1)} copy(bf16[1,64,2048]{1,0,2:T(2,128)(2,1)} %bitcast.112) | data formatting | bytes 524288 | tf_op jit(solution)/shard_map/all_to_all | solution.py:73
  66.8 24.2 %all-gather.9.cloned.1.call-done = bf16[2048,1,768]{2,0,1:T(8,128)(2,1)} async-done(((bf16[256,1,768]{2,0,1:T(8,128)(2,1)}), bf16[2048,1,768]{2,0,1:T(8,128)(2,1)}) %all-gather.9.cloned.1.call-update) | async-done | bytes 3145744 | tf_op jit(solution)/shard_map/all_gather | solution.py:30
  94.1 35.6 %all-gather.11.cloned.1.call-done = bf16[2048,1,768]{2,0,1:T(8,128)(2,1)} async-done(((bf16[256,1,768]{2,0,1:T(8,128)(2,1)}), bf16[2048,1,768]{2,0,1:T(8,128)(2,1)}) %all-gather.11.cloned.1.call-update) | async-done | bytes 3145744 | tf_op jit(solution)/shard_map/all_gather | solution.py:31
  133.9 3.8 %reduce.8 = bf16[64,2048]{1,0:T(8,128)(2,1)} reduce(bf16[64,1,2048]{2,1,0:T(2,128)(2,1)} %bitcast.123, bf16[]{:T(256)} %broadcast.134), dimensions={1}, to_apply=%bitcast.109.reduce_sub_computation | reduce | bytes 524290
  139.5 4.2 %all-to-all-start.1 = ((bf16[4,2,16384]{2,1,0:T(2,128)(2,1)}), bf16[4,2,16384]{2,1,0:T(2,128)(2,1)}, u32[]{:S(2)}, u32[]{:S(2)}) async-start(bf16[4,2,16384]{2,1,0:T(2,128)(2,1)} %reshape.297), calls=%async_computation.1 | async-start | bytes 524288 | tf_op jit(solution)/shard_map/all_to_all | solution.py:12
  143.8 5.8 %all-to-all-done.1 = bf16[4,2,16384]{2,1,0:T(2,128)(2,1)} async-done(((bf16[4,2,16384]{2,1,0:T(2,128)(2,1)}), bf16[4,2,16384]{2,1,0:T(2,128)(2,1)}, u32[]{:S(2)}, u32[]{:S(2)}) %all-to-all-start.1) | async-done | bytes 262176 | tf_op jit(solution)/shard_map/all_to_all | solution.py:12
  151.5 5.1 %scatter_custom_fusion = f32[768,2048]{1,0:T(8,128)} fusion(s32[64]{0:T(128)S(1)} %fusion.41, f32[]{:T(128)} %constant.5.clone.1, bf16[1,64,2048]{2,0,1:T(2,128)(2,1)} %bitcast.122, f32[64]{0:T(128)S(1)} %broadcast_select_fusion.1), kind=kCustom, calls=%fused_computation.19 | custom fusion | flops 393216 | bytes 6554116 | tf_op jit(solution)/shard_map/scatter-add | solution.py:48
  156.6 7.9 %convert_subtract_fusion = f32[768,2048]{1,0:T(8,128)} fusion(f32[768,2048]{1,0:T(8,128)} %scatter_custom_fusion, bf16[768,2048]{1,0:T(8,128)(2,1)} %param.9), kind=kLoop, calls=%fused_computation.4 | loop fusion | flops 3145728 | bytes 15728640 | tf_op jit(solution)/shard_map/sub | solution.py:50
  164.4 4.6 %gather_fusion.1 = f32[64,2048]{1,0:T(8,128)} fusion(f32[768,2048]{1,0:T(8,128)} %convert_subtract_fusion, s32[1024]{0:T(1024)S(1)} %pad_clamp_fusion), kind=kCustom, calls=%fused_computation.1 | custom fusion | bytes 1048832 | tf_op jit(solution)/shard_map/gather | solution.py:51
  170.8 4.1 %all-to-all-start.2 = ((bf16[4,16,2048]{2,1,0:T(8,128)(2,1)}), bf16[4,16,2048]{2,1,0:T(8,128)(2,1)}, u32[]{:S(2)}, u32[]{:S(2)}) async-start(bf16[4,16,2048]{2,1,0:T(8,128)(2,1)} %multiply_convert_fusion), calls=%async_computation.2 | async-start | bytes 524288 | tf_op jit(solution)/shard_map/all_to_all | solution.py:8
  174.9 16.5 %all-gather.2 = bf16[512,768]{1,0:T(8,128)(2,1)} all-gather(bf16[64,768]{1,0:T(8,128)(2,1)S(1)} %get-tuple-element.28), channel_id=4, replica_groups=mesh['dp'=8,'expert'=4] {'dp'}, dimensions={0}, use_global_device_ids=true | all-gather | bytes 884736 | tf_op jit(solution)/shard_map/all_gather | solution.py:76
  197.7 3.8 %reduce.9 = bf16[64,2048]{1,0:T(8,128)(2,1)} reduce(bf16[64,1,2048]{2,1,0:T(2,128)(2,1)} %bitcast.124, bf16[]{:T(256)} %broadcast.134), dimensions={1}, to_apply=%bitcast.108.reduce_sub_computation | reduce | bytes 524290
  203.4 4.2 %all-to-all-start.3 = ((bf16[4,2,16384]{2,1,0:T(2,128)(2,1)}), bf16[4,2,16384]{2,1,0:T(2,128)(2,1)}, u32[]{:S(2)}, u32[]{:S(2)}) async-start(bf16[4,2,16384]{2,1,0:T(2,128)(2,1)} %reshape.299), calls=%async_computation.3 | async-start | bytes 524288 | tf_op jit(solution)/shard_map/all_to_all | solution.py:12
  207.6 16.5 %all-gather = bf16[512,768]{1,0:T(8,128)(2,1)S(1)} all-gather(bf16[64,768]{1,0:T(8,128)(2,1)} %copy-done.4), channel_id=2, replica_groups=mesh['dp'=8,'expert'=4] {'dp'}, dimensions={0}, use_global_device_ids=true | all-gather | bytes 884736 | tf_op jit(solution)/shard_map/all_gather | solution.py:77
  231.8 13.3 %reduce.11 = bf16[2048,64]{1,0:T(8,128)(2,1)} reduce(bf16[2048,1,64]{2,1,0:T(2,128)(2,1)} %bitcast.115, bf16[]{:T(256)} %broadcast.134), dimensions={1}, to_apply=%bitcast.88.reduce_sub_computation | reduce | bytes 524290
  247.3 4.1 %all-to-all-start.5 = ((bf16[8,2,8192]{2,1,0:T(2,128)(2,1)}), bf16[8,2,8192]{2,1,0:T(2,128)(2,1)}, u32[]{:S(2)}, u32[]{:S(2)}) async-start(bf16[8,2,8192]{2,1,0:T(2,128)(2,1)} %reshape.303), calls=%async_computation.5 | async-start | bytes 524288 | tf_op jit(solution)/shard_map/all_to_all | solution.py:74
  251.3 19.9 %all-gather.1 = bf16[512,768]{1,0:T(8,128)(2,1)S(1)} all-gather(bf16[64,768]{1,0:T(8,128)(2,1)S(1)} %get-tuple-element.25), channel_id=3, replica_groups=mesh['dp'=8,'expert'=4] {'dp'}, dimensions={0}, use_global_device_ids=true | all-gather | bytes 884736 | tf_op jit(solution)/shard_map/all_gather | solution.py:78
  277.5 5.1 %scatter_custom_fusion.1 = f32[768,2048]{1,0:T(8,128)} fusion(s32[64]{0:T(128)S(1)} %fusion.41, f32[]{:T(128)} %constant.5.clone.1, bf16[1,64,2048]{2,0,1:T(2,128)(2,1)} %bitcast.125), kind=kCustom, calls=%fused_computation.17 | custom fusion | flops 262144 | bytes 6553604 | tf_op jit(solution)/shard_map/scatter-add | solution.py:68
  282.5 4.9 %convert_element_type.75 = bf16[768,2048]{1,0:T(8,128)(2,1)} convert(f32[768,2048]{1,0:T(8,128)} %scatter_custom_fusion.1) | non-fusion elementwise | flops 1572864 | bytes 9437184 | tf_op jit(solution)/shard_map/convert_element_type | solution.py:69
  (75 shorter events, 68.6 us)
Async XLA Ops:
  7.2 3.0 copy-start
  7.2 10.4 %copy-start.5 = (s32[1,4,1,16]{3,2,1,0:T(1,128)S(1)}, s32[1,4,1,16]{3,2,1,0:T(1,128)}, u32[]{:S(2)}) copy-start(s32[1,4,1,16]{3,2,1,0:T(1,128)} %param.10) | copy-start | bytes 772
  7.2 3.8 %copy-start.7 = (s32[1,4,1]{1,2,0:T(1,128)S(1)}, s32[1,4,1]{1,2,0:T(1,128)}, u32[]{:S(2)}) copy-start(s32[1,4,1]{1,2,0:T(1,128)} %param.11) | copy-start | bytes 52
  7.2 56.3 %all-gather.7.cloned.1.call-start = ((), (), s32[]{:S(2)}) async-start(), calls=%async_computation.6 | async-start | bytes 3538944 | tf_op jit(solution)/shard_map/all_gather | solution.py:29
  7.9 83.0 %all-gather.9.cloned.1.call-start = ((), (), s32[]{:S(2)}) async-start(), calls=%async_computation.7 | async-start | bytes 3538944 | tf_op jit(solution)/shard_map/all_gather | solution.py:30
  8.7 121.0 %all-gather.11.cloned.1.call-start = ((), (), s32[]{:S(2)}) async-start(), calls=%async_computation.8 | async-start | bytes 3538944 | tf_op jit(solution)/shard_map/all_gather | solution.py:31
  10.9 34.9 %copy-start.6 = (f32[1,4,1,16]{3,2,1,0:T(1,128)S(1)}, f32[1,4,1,16]{3,2,1,0:T(1,128)}, u32[]{:S(2)}) copy-start(f32[1,4,1,16]{3,2,1,0:T(1,128)} %param.12) | copy-start | bytes 772
  11.8 10.6 %all-to-all-start = ((bf16[4,16,2048]{2,1,0:T(8,128)(2,1)}), bf16[4,16,2048]{2,1,0:T(8,128)(2,1)S(1)}, u32[]{:S(2)}, u32[]{:S(2)}) async-start(bf16[4,16,2048]{2,1,0:T(8,128)(2,1)} %broadcast_multiply_fusion), calls=%async_computation | async-start | bytes 524288 | tf_op jit(solution)/shard_map/all_to_all | solution.py:8
  40.3 14.7 %all-to-all-start.4 = ((bf16[8,2,8192]{2,1,0:T(2,128)(2,1)}), bf16[8,2,8192]{2,1,0:T(2,128)(2,1)}, u32[]{:S(2)}, u32[]{:S(2)}) async-start(bf16[8,2,8192]{2,1,0:T(2,128)(2,1)} %reshape.301), calls=%async_computation.4 | async-start | bytes 524288 | tf_op jit(solution)/shard_map/all_to_all | solution.py:73
  94.1 49.6 %copy-start.3 = (bf16[8,8,8,256]{3,2,1,0:T(8,128)(2,1)S(1)}, bf16[8,8,8,256]{3,2,1,0:T(8,128)(2,1)}, u32[]{:S(2)}) copy-start(bf16[8,8,8,256]{3,2,1,0:T(8,128)(2,1)} %copy.49) | copy-start | bytes 786436
  139.5 10.2 %all-to-all-start.1 = ((bf16[4,2,16384]{2,1,0:T(2,128)(2,1)}), bf16[4,2,16384]{2,1,0:T(2,128)(2,1)}, u32[]{:S(2)}, u32[]{:S(2)}) async-start(bf16[4,2,16384]{2,1,0:T(2,128)(2,1)} %reshape.297), calls=%async_computation.1 | async-start | bytes 524288 | tf_op jit(solution)/shard_map/all_to_all | solution.py:12
  170.8 20.5 %all-to-all-start.2 = ((bf16[4,16,2048]{2,1,0:T(8,128)(2,1)}), bf16[4,16,2048]{2,1,0:T(8,128)(2,1)}, u32[]{:S(2)}, u32[]{:S(2)}) async-start(bf16[4,16,2048]{2,1,0:T(8,128)(2,1)} %multiply_convert_fusion), calls=%async_computation.2 | async-start | bytes 524288 | tf_op jit(solution)/shard_map/all_to_all | solution.py:8
  191.4 3.0 copy-start.2
  191.4 4.1 %copy-start.1 = (bf16[2048,1,768]{2,0,1:T(8,128)(2,1)S(1)}, bf16[2048,1,768]{2,0,1:T(8,128)(2,1)}, u32[]{:S(2)}) copy-start(bf16[2048,1,768]{2,0,1:T(8,128)(2,1)} %all-gather.7.cloned.1.call-done) | copy-start | bytes 9437188
  194.2 2.3 copy-start.4
  203.4 43.9 %all-to-all-start.3 = ((bf16[4,2,16384]{2,1,0:T(2,128)(2,1)}), bf16[4,2,16384]{2,1,0:T(2,128)(2,1)}, u32[]{:S(2)}, u32[]{:S(2)}) async-start(bf16[4,2,16384]{2,1,0:T(2,128)(2,1)} %reshape.299), calls=%async_computation.3 | async-start | bytes 524288 | tf_op jit(solution)/shard_map/all_to_all | solution.py:12
  247.3 40.2 %all-to-all-start.5 = ((bf16[8,2,8192]{2,1,0:T(2,128)(2,1)}), bf16[8,2,8192]{2,1,0:T(2,128)(2,1)}, u32[]{:S(2)}, u32[]{:S(2)}) async-start(bf16[8,2,8192]{2,1,0:T(2,128)(2,1)} %reshape.303), calls=%async_computation.5 | async-start | bytes 524288 | tf_op jit(solution)/shard_map/all_to_all | solution.py:74
Sparse Core Ops, SparseCore 0:
  9.6 40.9 all-gather.6
  52.3 38.6 all-gather.8
  92.6 37.1 all-gather.10
where the time goes:
time: 307 us; the launch traced here: 305 us
  waiting for transfers between devices  80.1 us (26%)
  other arithmetic  62 us (20%)
  blocking collectives  52.9 us (17%)
  local copies, waits for them, and re-layouts  50.3 us (16%)
  starting transfers between devices  26.7 us (9%)
  matrix products  19.3 us (6%)
  between operations  13.9 us (5%)
    all_gather x1, waiting for transfers between devices, on_device(): lax.all_gather(down_weight, 'dp', axis=0, tiled=True)  35.6 us
    unnamed x6, other arithmetic  35.6 us
    unnamed x32, local copies, waits for them, and re-layouts  31.1 us
    all_gather x1, waiting for transfers between devices, on_device(): lax.all_gather(up_weight, 'dp', axis=0, tiled=True)  24.2 us
    all_gather x1, blocking collectives, on_device(): up_piece = lax.all_gather(up_grad, 'dp', axis=1, tiled=True)  19.9 us
    all_gather x1, blocking collectives, on_device(): gate_piece = lax.all_gather(gate_grad, 'dp', axis=1, tiled=True)  16.5 us
    all_gather x1, blocking collectives, on_device(): hidden_piece = lax.all_gather(hidden, 'dp', axis=1, tiled=True)  16.5 us
    all_to_all x2, starting transfers between devices, to_owners(): lax.all_to_all(block, 'expert', split_axis=0, concat_axis=1, tiled=True)  9.24 us
  transfers between devices with their start and end apart: 9, of which 5 were waited for; matrix products, arithmetic and copies ran while one was open for 25% of the time, Pallas kernels for 0%

commit v1 on v0

--- a/solution.py
+++ b/solution.py
@@ -73,16 +73,27 @@
         lax.all_to_all(expert_rows, "dp", split_axis=2, concat_axis=1, tiled=True),
         lax.all_to_all(owner_grad, "dp", split_axis=2, concat_axis=1, tiled=True),
     )
-    hidden_piece = lax.all_gather(hidden, "dp", axis=1, tiled=True)
     gate_piece = lax.all_gather(gate_grad, "dp", axis=1, tiled=True)
     up_piece = lax.all_gather(up_grad, "dp", axis=1, tiled=True)
     gate_sum = jnp.einsum(
         "erd,erf->def", rows_every, gate_piece, preferred_element_type=jnp.float32
     )
     up_sum = jnp.einsum("erd,erf->def", rows_every, up_piece, preferred_element_type=jnp.float32)
-    down_sum = jnp.einsum(
-        "erd,erf->def", grad_every, hidden_piece, preferred_element_type=jnp.float32
-    )
+    count, place, span = (lax.axis_size("dp"), lax.axis_index("dp"), hidden.shape[1])
+    right = [(i, (i + 1) % count) for i in range(count)]
+    held, down_sum = (hidden, None)
+    for step in range(count):
+        arriving = lax.ppermute(held, "dp", right) if step < count - 1 else None
+        absorb = jnp.einsum(
+            "erd,erf->def",
+            lax.dynamic_slice_in_dim(
+                grad_every, (place - step) % count * span, held.shape[1], axis=1
+            ),
+            held,
+            preferred_element_type=jnp.float32,
+        )
+        down_sum = absorb if down_sum is None else down_sum + absorb
+        held = arriving
     gate_gradient = gate_sum * factor
     up_gradient = up_sum * factor
     down_gradient = down_sum * factor

time: 307 us -> 284 us (0.925)
  local copies, waits for them, and re-layouts: 50.3 us -> 25.3 us
  waiting for transfers between devices: 80.1 us -> 105 us
  blocking collectives: 52.9 us -> 35.4 us
  other arithmetic: 62 us -> 53 us
  matrix products: 19.3 us -> 24.2 us
    all_gather x1 -> x0, blocking collectives: 16.5 us -> none  [on_device(): hidden_piece = lax.all_gather(hidden, 'dp', axis=1, tiled=True)]
    unnamed x32 -> x46, local copies, waits for them, and re-layouts: 31.1 us -> 15.4 us
    all_gather x1, waiting for transfers between devices: 24.2 us -> 37.9 us  [on_device(): lax.all_gather(up_weight, 'dp', axis=0, tiled=True)]
    all_gather x1, waiting for transfers between devices: 0.01 us -> 12.8 us  [on_device(): lax.all_gather(gate_weight, 'dp', axis=0, tiled=True)]
    ppermute x0 -> x7, waiting for transfers between devices: none -> 10.4 us  [on_device(): arriving = lax.ppermute(held, 'dp', right) if step < count - 1 else None]
    all_to_all x1, waiting for transfers between devices: 8.38 us -> 0.01 us  [on_device(): lax.all_to_all(expert_rows, 'dp', split_axis=2, concat_axis=1, tiled=True)]
    unnamed x6, other arithmetic: 35.6 us -> 28.9 us
    dot_general x1 -> x8, matrix products: 2.43 us -> 7.85 us  [on_device(): jnp.einsum('erd,erf->def', lax.dynamic_slice_in_dim(grad_every, (place -...]
  transfers between devices with their start and end apart: 9 -> 16, of which waited for: 5 -> 8; matrix products, arithmetic and copies ran while one was open for 25% -> 34% of each run, Pallas kernels for 0% -> 0%
where the time goes in v1:
time: 284 us; the launch traced here: 283 us
  waiting for transfers between devices  105 us (37%)
  other arithmetic  53 us (19%)
  blocking collectives  35.4 us (12%)
  starting transfers between devices  25.4 us (9%)
  local copies, waits for them, and re-layouts  25.3 us (9%)
  matrix products  24.2 us (9%)
  between operations  14.2 us (5%)
    all_gather x1, waiting for transfers between devices, on_device(): lax.all_gather(up_weight, 'dp', axis=0, tiled=True)  37.9 us
    all_gather x1, waiting for transfers between devices, on_device(): lax.all_gather(down_weight, 'dp', axis=0, tiled=True)  35.6 us
    unnamed x6, other arithmetic  28.9 us
    all_gather x1, blocking collectives, on_device(): up_piece = lax.all_gather(up_grad, 'dp', axis=1, tiled=True)  20 us
    all_gather x1, blocking collectives, on_device(): gate_piece = lax.all_gather(gate_grad, 'dp', axis=1, tiled=True)  15.4 us
    unnamed x46, local copies, waits for them, and re-layouts  15.4 us
    all_gather x1, waiting for transfers between devices, on_device(): lax.all_gather(gate_weight, 'dp', axis=0, tiled=True)  12.8 us
    ppermute x7, waiting for transfers between devices, on_device(): arriving = lax.ppermute(held, 'dp', right) if step < count - 1 else None  10.4 us
  transfers between devices with their start and end apart: 16, of which 8 were waited for; matrix products, arithmetic and copies ran while one was open for 34% of the time, Pallas kernels for 0%

profile of v1, /device:TPU:0, one launch (start us, length us, event | category | flops | bytes accessed | tf_op | source)
XLA Modules:
  0.0 283.0 jit_solution(1251254520554583286)
XLA Ops:
  11.8 5.2 %all-to-all-start = ((bf16[4,16,2048]{2,1,0:T(8,128)(2,1)}), bf16[4,16,2048]{2,1,0:T(8,128)(2,1)S(1)}, u32[]{:S(2)}, u32[]{:S(2)}) async-start(bf16[4,16,2048]{2,1,0:T(8,128)(2,1)} %broadcast_multiply_fusion), calls=%async_computation | async-start | bytes 524288 | tf_op jit(solution)/shard_map/all_to_all | solution.py:8
  23.7 11.6 %reduce.10 = bf16[2048,64]{1,0:T(8,128)(2,1)S(1)} reduce(bf16[2048,1,64]{2,1,0:T(2,128)(2,1)S(1)} %bitcast.159, bf16[]{:T(256)} %broadcast.146), dimensions={1}, to_apply=%bitcast.132.reduce_sub_computation | reduce | bytes 524290
  36.4 4.9 %all-to-all-start.4 = ((bf16[8,2,8192]{2,1,0:T(2,128)(2,1)}), bf16[8,2,8192]{2,1,0:T(2,128)(2,1)S(1)}, u32[]{:S(2)}, u32[]{:S(2)}) async-start(bf16[8,2,8192]{2,1,0:T(2,128)(2,1)} %reshape.366), calls=%async_computation.4 | async-start | bytes 524288 | tf_op jit(solution)/shard_map/all_to_all | solution.py:73
  41.3 12.8 %all-gather.6.cloned.1.call-done = bf16[2048,1,768]{2,0,1:T(8,128)(2,1)} async-done(((bf16[256,1,768]{2,0,1:T(8,128)(2,1)}), bf16[2048,1,768]{2,0,1:T(8,128)(2,1)}) %all-gather.6.cloned.1.call-update) | async-done | bytes 3145744 | tf_op jit(solution)/shard_map/all_gather | solution.py:29
  56.6 37.9 %all-gather.8.cloned.1.call-done = bf16[2048,1,768]{2,0,1:T(8,128)(2,1)} async-done(((bf16[256,1,768]{2,0,1:T(8,128)(2,1)}), bf16[2048,1,768]{2,0,1:T(8,128)(2,1)}) %all-gather.8.cloned.1.call-update) | async-done | bytes 3145744 | tf_op jit(solution)/shard_map/all_gather | solution.py:30
  94.5 3.2 %multiply_convert_fusion.3 = (bf16[64,768]{1,0:T(8,128)(2,1)S(1)}, f32[64,768]{1,0:T(8,128)}) fusion(f32[64,768]{1,0:T(8,128)S(1)} %fusion.10, bf16[64,2048]{1,0:T(8,128)(2,1)S(1)} %bitcast.163, bf16[2048,1,768]{2,0,1:T(8,128)(2,1)} %all-gather.8.cloned.1.call-done), kind=kOutput, calls=%fused_computation.51 | convolution fusion | flops 201621504 | bytes 3899392 | tf_op jit(solution)/shard_map/erd,def->erf/dot_general | solution.py:36
  97.7 35.6 %all-gather.10.cloned.1.call-done = bf16[2048,1,768]{2,0,1:T(8,128)(2,1)} async-done(((bf16[256,1,768]{2,0,1:T(8,128)(2,1)}), bf16[2048,1,768]{2,0,1:T(8,128)(2,1)}) %all-gather.10.cloned.1.call-update) | async-done | bytes 3145744 | tf_op jit(solution)/shard_map/all_gather | solution.py:31
  140.0 3.6 %all-to-all-start.1 = ((bf16[4,2,16384]{2,1,0:T(2,128)(2,1)}), bf16[4,2,16384]{2,1,0:T(2,128)(2,1)S(1)}, u32[]{:S(2)}, u32[]{:S(2)}) async-start(bf16[4,2,16384]{2,1,0:T(2,128)(2,1)} %reshape.362), calls=%async_computation.1 | async-start | bytes 524288 | tf_op jit(solution)/shard_map/all_to_all | solution.py:12
  145.7 4.0 %all-to-all-done.1 = bf16[4,2,16384]{2,1,0:T(2,128)(2,1)S(1)} async-done(((bf16[4,2,16384]{2,1,0:T(2,128)(2,1)}), bf16[4,2,16384]{2,1,0:T(2,128)(2,1)S(1)}, u32[]{:S(2)}, u32[]{:S(2)}) %all-to-all-start.1) | async-done | bytes 262176 | tf_op jit(solution)/shard_map/all_to_all | solution.py:12
  150.7 5.3 %scatter_custom_fusion = f32[768,2048]{1,0:T(8,128)} fusion(s32[64]{0:T(128)S(1)} %fusion.74, f32[]{:T(128)} %constant.67.clone.1, bf16[1,64,2048]{2,0,1:T(2,128)(2,1)} %bitcast.169, f32[64]{0:T(128)S(1)} %broadcast_select_fusion.1), kind=kCustom, calls=%fused_computation.19 | custom fusion | flops 393216 | bytes 6554116 | tf_op jit(solution)/shard_map/scatter-add | solution.py:48
  155.9 6.9 %convert_subtract_fusion = f32[768,2048]{1,0:T(8,128)} fusion(f32[768,2048]{1,0:T(8,128)} %scatter_custom_fusion, bf16[768,2048]{1,0:T(8,128)(2,1)S(1)} %copy-done.3), kind=kLoop, calls=%fused_computation.4 | loop fusion | flops 3145728 | bytes 15728640 | tf_op jit(solution)/shard_map/sub | solution.py:50
  162.8 3.8 %gather_fusion.1 = f32[64,2048]{1,0:T(8,128)S(1)} fusion(f32[768,2048]{1,0:T(8,128)} %convert_subtract_fusion, s32[1024]{0:T(1024)S(1)} %pad_clamp_fusion), kind=kCustom, calls=%fused_computation.1 | custom fusion | bytes 1048832 | tf_op jit(solution)/shard_map/gather | solution.py:51
  167.4 3.4 %all-to-all-start.2 = ((bf16[4,16,2048]{2,1,0:T(8,128)(2,1)}), bf16[4,16,2048]{2,1,0:T(8,128)(2,1)S(1)}, u32[]{:S(2)}, u32[]{:S(2)}) async-start(bf16[4,16,2048]{2,1,0:T(8,128)(2,1)} %multiply_convert_fusion), calls=%async_computation.2 | async-start | bytes 524288 | tf_op jit(solution)/shard_map/all_to_all | solution.py:8
  171.0 6.1 %collective-permute-done.2 = bf16[1,64,768]{2,1,0:T(8,128)(2,1)} collective-permute-done((bf16[1,64,768]{2,1,0:T(8,128)(2,1)}, bf16[1,64,768]{2,1,0:T(8,128)(2,1)}, u32[]{:S(2)}, u32[]{:S(2)}) %collective-permute-start.2) | collective-permute-done | bytes 98336 | tf_op jit(solution)/shard_map/ppermute | solution.py:86
  180.6 3.0 %fusion.4 = f32[64,2048]{1,0:T(8,128)S(1)} fusion(bf16[64,768]{1,0:T(8,128)(2,1)S(1)} %get-tuple-element.25, bf16[2048,1,768]{2,0,1:T(8,128)(2,1)} %all-gather.8.cloned.1.call-done), kind=kOutput, calls=%fused_computation.9 | convolution fusion | flops 201326592 | bytes 3768320 | tf_op jit(solution)/shard_map/erf,def->erd/dot_general | solution.py:62
  188.3 4.1 %all-to-all-start.3 = ((bf16[4,2,16384]{2,1,0:T(2,128)(2,1)}), bf16[4,2,16384]{2,1,0:T(2,128)(2,1)S(1)}, u32[]{:S(2)}, u32[]{:S(2)}) async-start(bf16[4,2,16384]{2,1,0:T(2,128)(2,1)} %reshape.364), calls=%async_computation.3 | async-start | bytes 524288 | tf_op jit(solution)/shard_map/all_to_all | solution.py:12
  194.6 11.6 %reduce.11 = bf16[2048,64]{1,0:T(8,128)(2,1)S(1)} reduce(bf16[2048,1,64]{2,1,0:T(2,128)(2,1)S(1)} %bitcast.160, bf16[]{:T(256)} %broadcast.146), dimensions={1}, to_apply=%bitcast.134.reduce_sub_computation | reduce | bytes 524290
  207.3 15.4 %all-gather = bf16[512,768]{1,0:T(8,128)(2,1)S(1)} all-gather(bf16[64,768]{1,0:T(8,128)(2,1)S(1)} %copy-done.9), channel_id=2, replica_groups=mesh['dp'=8,'expert'=4] {'dp'}, dimensions={0}, use_global_device_ids=true | all-gather | bytes 884736 | tf_op jit(solution)/shard_map/all_gather | solution.py:76
  222.7 3.4 %all-to-all-start.5 = ((bf16[8,2,8192]{2,1,0:T(2,128)(2,1)}), bf16[8,2,8192]{2,1,0:T(2,128)(2,1)S(1)}, u32[]{:S(2)}, u32[]{:S(2)}) async-start(bf16[8,2,8192]{2,1,0:T(2,128)(2,1)} %reshape.368), calls=%async_computation.5 | async-start | bytes 524288 | tf_op jit(solution)/shard_map/all_to_all | solution.py:74
  226.1 20.0 %all-gather.1 = bf16[512,768]{1,0:T(8,128)(2,1)S(1)} all-gather(bf16[64,768]{1,0:T(8,128)(2,1)S(1)} %copy-done.7), channel_id=3, replica_groups=mesh['dp'=8,'expert'=4] {'dp'}, dimensions={0}, use_global_device_ids=true | all-gather | bytes 884736 | tf_op jit(solution)/shard_map/all_gather | solution.py:77
  248.6 3.6 %collective-permute-done.4 = bf16[1,64,768]{2,1,0:T(8,128)(2,1)S(1)} collective-permute-done((bf16[1,64,768]{2,1,0:T(8,128)(2,1)}, bf16[1,64,768]{2,1,0:T(8,128)(2,1)S(1)}, u32[]{:S(2)}, u32[]{:S(2)}) %collective-permute-start.4) | collective-permute-done | bytes 98336 | tf_op jit(solution)/shard_map/ppermute | solution.py:86
  254.6 4.5 %scatter_custom_fusion.1 = f32[768,2048]{1,0:T(8,128)} fusion(s32[64]{0:T(128)S(1)} %fusion.74, f32[]{:T(128)} %constant.67.clone.1, bf16[1,64,2048]{2,0,1:T(2,128)(2,1)S(1)} %bitcast.172), kind=kCustom, calls=%fused_computation.17 | custom fusion | flops 262144 | bytes 6815748 | tf_op jit(solution)/shard_map/scatter-add | solution.py:68
  259.1 4.9 %convert_element_type.75 = bf16[768,2048]{1,0:T(8,128)(2,1)} convert(f32[768,2048]{1,0:T(8,128)} %scatter_custom_fusion.1) | non-fusion elementwise | flops 1572864 | bytes 9437184 | tf_op jit(solution)/shard_map/convert_element_type | solution.py:69
  273.4 3.0 %copy.48 = f32[256,1,768]{2,1,0:T(1,128)} copy(f32[256,1,768]{0,2,1:T(8,128)} %fusion.32) | data formatting | bytes 1572864
  (109 shorter events, 51.1 us)
Async XLA Ops:
  7.2 10.4 %copy-start.12 = (s32[1,4,1,16]{3,2,1,0:T(1,128)S(1)}, s32[1,4,1,16]{3,2,1,0:T(1,128)}, u32[]{:S(2)}) copy-start(s32[1,4,1,16]{3,2,1,0:T(1,128)} %param.10) | copy-start | bytes 772
  7.2 11.7 %copy-start.13 = (f32[1,4,1,16]{3,2,1,0:T(1,128)S(1)}, f32[1,4,1,16]{3,2,1,0:T(1,128)}, u32[]{:S(2)}) copy-start(f32[1,4,1,16]{3,2,1,0:T(1,128)} %param.12) | copy-start | bytes 772
  7.2 46.9 %all-gather.6.cloned.1.call-start = ((), (), s32[]{:S(2)}) async-start(), calls=%async_computation.6 | async-start | bytes 3538944 | tf_op jit(solution)/shard_map/all_gather | solution.py:29
  7.9 86.6 %all-gather.8.cloned.1.call-start = ((), (), s32[]{:S(2)}) async-start(), calls=%async_computation.7 | async-start | bytes 3538944 | tf_op jit(solution)/shard_map/all_gather | solution.py:30
  8.7 124.6 %all-gather.10.cloned.1.call-start = ((), (), s32[]{:S(2)}) async-start(), calls=%async_computation.8 | async-start | bytes 3538944 | tf_op jit(solution)/shard_map/all_gather | solution.py:31
  11.8 10.6 %all-to-all-start = ((bf16[4,16,2048]{2,1,0:T(8,128)(2,1)}), bf16[4,16,2048]{2,1,0:T(8,128)(2,1)S(1)}, u32[]{:S(2)}, u32[]{:S(2)}) async-start(bf16[4,16,2048]{2,1,0:T(8,128)(2,1)} %broadcast_multiply_fusion), calls=%async_computation | async-start | bytes 524288 | tf_op jit(solution)/shard_map/all_to_all | solution.py:8
  36.4 103.6 %all-to-all-start.4 = ((bf16[8,2,8192]{2,1,0:T(2,128)(2,1)}), bf16[8,2,8192]{2,1,0:T(2,128)(2,1)S(1)}, u32[]{:S(2)}, u32[]{:S(2)}) async-start(bf16[8,2,8192]{2,1,0:T(2,128)(2,1)} %reshape.366), calls=%async_computation.4 | async-start | bytes 524288 | tf_op jit(solution)/shard_map/all_to_all | solution.py:73
  56.6 76.7 %copy-start.5 = (f32[64,768]{1,0:T(8,128)}, f32[64,768]{1,0:T(8,128)S(1)}, u32[]{:S(2)}) copy-start(f32[64,768]{1,0:T(8,128)S(1)} %fusion.10) | copy-start | bytes 589828
  139.8 5.9 %collective-permute-start = (bf16[1,64,768]{2,1,0:T(8,128)(2,1)S(1)}, bf16[1,64,768]{2,1,0:T(8,128)(2,1)}, u32[]{:S(2)}, u32[]{:S(2)}) collective-permute-start(bf16[1,64,768]{2,1,0:T(8,128)(2,1)S(1)} %bitcast.186), channel_id=1, source_target_pairs={{0,4},{4,8},{8,12},{12,16},{16,20},{20,24},{24,28},{28,0},{1,5},{5... | collective-permute-start | bytes 294920 | tf_op jit(solution)/shard_map/ppermute | solution.py:86
  140.0 9.7 %all-to-all-start.1 = ((bf16[4,2,16384]{2,1,0:T(2,128)(2,1)}), bf16[4,2,16384]{2,1,0:T(2,128)(2,1)S(1)}, u32[]{:S(2)}, u32[]{:S(2)}) async-start(bf16[4,2,16384]{2,1,0:T(2,128)(2,1)} %reshape.362), calls=%async_computation.1 | async-start | bytes 524288 | tf_op jit(solution)/shard_map/all_to_all | solution.py:12
  145.7 25.1 %collective-permute-start.1 = (bf16[1,64,768]{2,1,0:T(8,128)(2,1)}, bf16[1,64,768]{2,1,0:T(8,128)(2,1)}, u32[]{:S(2)}, u32[]{:S(2)}) collective-permute-start(bf16[1,64,768]{2,1,0:T(8,128)(2,1)} %collective-permute-done), channel_id=1, source_target_pairs={{0,4},{4,8},{8,12},{12,16},{16,20},{20,24},{24,28},{28,0},{1,5},{5... | collective-permute-start | bytes 294920 | tf_op jit(solution)/shard_map/ppermute | solution.py:86
  167.4 9.6 %all-to-all-start.2 = ((bf16[4,16,2048]{2,1,0:T(8,128)(2,1)}), bf16[4,16,2048]{2,1,0:T(8,128)(2,1)S(1)}, u32[]{:S(2)}, u32[]{:S(2)}) async-start(bf16[4,16,2048]{2,1,0:T(8,128)(2,1)} %multiply_convert_fusion), calls=%async_computation.2 | async-start | bytes 524288 | tf_op jit(solution)/shard_map/all_to_all | solution.py:8
  170.8 6.2 %collective-permute-start.2 = (bf16[1,64,768]{2,1,0:T(8,128)(2,1)}, bf16[1,64,768]{2,1,0:T(8,128)(2,1)}, u32[]{:S(2)}, u32[]{:S(2)}) collective-permute-start(bf16[1,64,768]{2,1,0:T(8,128)(2,1)} %collective-permute-done.1), channel_id=1, source_target_pairs={{0,4},{4,8},{8,12},{12,16},{16,20},{20,24},{24,28},{28,0},{1,5},{5... | collective-permute-start | bytes 294920 | tf_op jit(solution)/shard_map/ppermute | solution.py:86
  177.0 69.0 %collective-permute-start.3 = (bf16[1,64,768]{2,1,0:T(8,128)(2,1)}, bf16[1,64,768]{2,1,0:T(8,128)(2,1)}, u32[]{:S(2)}, u32[]{:S(2)}) collective-permute-start(bf16[1,64,768]{2,1,0:T(8,128)(2,1)} %collective-permute-done.2), channel_id=1, source_target_pairs={{0,4},{4,8},{8,12},{12,16},{16,20},{20,24},{24,28},{28,0},{1,5},{5... | collective-permute-start | bytes 294920 | tf_op jit(solution)/shard_map/ppermute | solution.py:86
  177.8 5.9 %copy-start.2 = (bf16[2048,1,768]{2,0,1:T(8,128)(2,1)S(1)}, bf16[2048,1,768]{2,0,1:T(8,128)(2,1)}, u32[]{:S(2)}) copy-start(bf16[2048,1,768]{2,0,1:T(8,128)(2,1)} %all-gather.6.cloned.1.call-done) | copy-start | bytes 9437188
  185.1 22.1 %copy-start.9 = (bf16[64,768]{1,0:T(8,128)(2,1)S(1)}, bf16[64,768]{1,0:T(8,128)(2,1)}, u32[]{:S(2)}) copy-start(bf16[64,768]{1,0:T(8,128)(2,1)} %copy-done.8) | copy-start | bytes 294916
  187.4 38.7 %copy-start.7 = (bf16[64,768]{1,0:T(8,128)(2,1)S(1)}, bf16[64,768]{1,0:T(8,128)(2,1)}, u32[]{:S(2)}) copy-start(bf16[64,768]{1,0:T(8,128)(2,1)} %copy-done.6) | copy-start | bytes 294916
  188.3 34.4 %all-to-all-start.3 = ((bf16[4,2,16384]{2,1,0:T(2,128)(2,1)}), bf16[4,2,16384]{2,1,0:T(2,128)(2,1)S(1)}, u32[]{:S(2)}, u32[]{:S(2)}) async-start(bf16[4,2,16384]{2,1,0:T(2,128)(2,1)} %reshape.364), calls=%async_computation.3 | async-start | bytes 524288 | tf_op jit(solution)/shard_map/all_to_all | solution.py:12
  222.7 41.4 %all-to-all-start.5 = ((bf16[8,2,8192]{2,1,0:T(2,128)(2,1)}), bf16[8,2,8192]{2,1,0:T(2,128)(2,1)S(1)}, u32[]{:S(2)}, u32[]{:S(2)}) async-start(bf16[8,2,8192]{2,1,0:T(2,128)(2,1)} %reshape.368), calls=%async_computation.5 | async-start | bytes 524288 | tf_op jit(solution)/shard_map/all_to_all | solution.py:74
  246.1 6.1 %collective-permute-start.4 = (bf16[1,64,768]{2,1,0:T(8,128)(2,1)}, bf16[1,64,768]{2,1,0:T(8,128)(2,1)S(1)}, u32[]{:S(2)}, u32[]{:S(2)}) collective-permute-start(bf16[1,64,768]{2,1,0:T(8,128)(2,1)} %collective-permute-done.3), channel_id=1, source_target_pairs={{0,4},{4,8},{8,12},{12,16},{16,20},{20,24},{24,28},{28,0},{1,5},{5... | collective-permute-start | bytes 294920 | tf_op jit(solution)/shard_map/ppermute | solution.py:86
  252.1 7.0 %copy-start.10 = (bf16[1,64,768]{2,1,0:T(8,128)(2,1)}, bf16[1,64,768]{2,1,0:T(8,128)(2,1)S(1)}, u32[]{:S(2)}) copy-start(bf16[1,64,768]{2,1,0:T(8,128)(2,1)S(1)} %collective-permute-done.4) | copy-start | bytes 294916
  252.1 11.9 %collective-permute-start.5 = (bf16[1,64,768]{2,1,0:T(8,128)(2,1)S(1)}, bf16[1,64,768]{2,1,0:T(8,128)(2,1)}, u32[]{:S(2)}, u32[]{:S(2)}) collective-permute-start(bf16[1,64,768]{2,1,0:T(8,128)(2,1)S(1)} %collective-permute-done.4), channel_id=1, source_target_pairs={{0,4},{4,8},{8,12},{12,16},{16,20},{20,24},{24,28},{28,0},{1,5},{5... | collective-permute-start | bytes 294920 | tf_op jit(solution)/shard_map/ppermute | solution.py:86
  264.1 8.2 %collective-permute-start.6 = (bf16[1,64,768]{2,1,0:T(8,128)(2,1)}, bf16[1,64,768]{2,1,0:T(8,128)(2,1)S(1)}, u32[]{:S(2)}, u32[]{:S(2)}) collective-permute-start(bf16[1,64,768]{2,1,0:T(8,128)(2,1)} %collective-permute-done.5), channel_id=1, source_target_pairs={{0,4},{4,8},{8,12},{12,16},{16,20},{20,24},{24,28},{28,0},{1,5},{5... | collective-permute-start | bytes 294920 | tf_op jit(solution)/shard_map/ppermute | solution.py:86
  269.4 7.1 %copy-start.1 = (bf16[768,2048]{1,0:T(8,128)(2,1)S(1)}, bf16[768,2048]{1,0:T(8,128)(2,1)}, u32[]{:S(2)}) copy-start(bf16[768,2048]{1,0:T(8,128)(2,1)} %param.8) | copy-start | bytes 9437188
  (7 other events, 24.9 us)
Sparse Core Ops, SparseCore 0:
  9.7 44.3 all-gather.5
  55.7 38.7 all-gather.7
  96.2 37.1 all-gather.9
